TPU v7x, 128 devices: a whole 4x4x4 slice. The times are simulated.
128 devices in a mesh: req: 8 (over y, core), exp: 16 (over x, z).
Axes of the slice: x: 4, y: 4, z: 4, core: 2. Of those that a mesh axis runs over, the one named last changes fastest.
Arguments:
- tokens: bfloat16 [49152, 1536], P(('req', 'exp')), may hold values from -30 to 30
- segment_lengths: int32 [8, 16], P('req'), may hold values from 1 to 3071, as said below
- segment_adapters: int32 [8, 16], P('req'), may hold values from 0 to 15
- routes: int32 [49152, 4], P(('req', 'exp')), may hold values from 0 to 31, all different within a row; in each aligned block of 384 rows (0 to 383, 384 to 767, ...) at most 64 rows name the same one
- gate_weights: float32 [49152, 4], P(('req', 'exp')), may hold values from 0.05 to 1
- attention_gain: float32 [1536], replicated, may hold values from 0.5 to 1.5
- attention_in: bfloat16 [1536, 2048], P(None, 'req'), may hold values from -5 to 5
- sink_logits: float32 [12], replicated, may hold values from 0 to 6
- attention_out: bfloat16 [1536, 1536], P(None, 'req'), may hold values from -0.15625 to 0.15625
- expert_gain: float32 [1536], replicated, may hold values from 0.5 to 1.5
- expert_gate_up: bfloat16 [32, 1536, 1536], P('exp'), may hold values from -0.15625 to 0.15625
- expert_down: bfloat16 [32, 768, 1536], P('exp'), may hold values from -0.21875 to 0.21875
- adapter_in_down: bfloat16 [16, 1536, 16], P('req'), may hold values from -0.15625 to 0.15625
- adapter_in_up: bfloat16 [16, 16, 2048], P('req'), may hold values from -0.625 to 0.625
- adapter_out_down: bfloat16 [16, 1536, 16], P('req'), may hold values from -0.15625 to 0.15625
- adapter_out_up: bfloat16 [16, 16, 1536], P('req'), may hold values from -0.625 to 0.625
- adapter_expert_down: bfloat16 [16, 1536, 16], P('req'), may hold values from -0.15625 to 0.15625
- adapter_expert_up: bfloat16 [16, 32, 16, 768], P('req', 'exp'), may hold values from -0.625 to 0.625
Outputs:
- layer_output: bfloat16 [49152, 1536], P(('req', 'exp'))
Inputs may be any that keep to these rules, and one draw needn't show every extreme that they name: `segment_lengths`: each row sums to 6144; entry 0 is the group's shared prompt of 1536 to 3071 tokens, the other entries are its requests, none longer than the prompt's most. `routes`: in each aligned block of 384 token rows (the rows of one device) no expert is named more than 64 times, a bound that some block reaches; a row names 4 different experts.
All inputs are finite; a program needn't handle non-finite values.
Results may differ from a plain program's by a relative error of at most 0.012.
The roundings to bfloat16 on the way count: a program that leaves them out, or rounds other values in their place, can miss the bound.
Values may be sent and summed in bfloat16 or wider, within the bound.
A program may use at most 128 MiB of HBM per device.

v0:
```python
import jax
import jax.numpy as jnp
from jax import lax
from jax.sharding import PartitionSpec as P

HEADS = 12
KVH = 2
HD = 128
EXPERTS = 32
WINDOW = 4096
CAP = 64
EPSILON = 1e-06
NEGATIVE = -1e30


def scaled_norm(inputs, gain):
    floats = inputs.astype(jnp.float32)
    inverse = lax.rsqrt(jnp.mean(floats * floats, axis=-1, keepdims=True) + EPSILON)
    return (floats * inverse * gain).astype(jnp.bfloat16)


def segment_of(positions, lengths):
    seg_ends = jnp.cumsum(lengths)
    return jnp.sum((positions[:, None] >= seg_ends[None, :]).astype(jnp.int32), axis=1)


def adapter_select(token_adapter, adapter_count, rank_size):
    owners = jnp.repeat(jnp.arange(adapter_count, dtype=jnp.int32), rank_size)
    return token_adapter[:, None] == owners[None, :]


def low_coords(inputs, select, first_factor):
    adapter_count, inner_width, rank_size = first_factor.shape
    joined = jnp.transpose(first_factor, (1, 0, 2)).reshape(inner_width, adapter_count * rank_size)
    coords = jnp.dot(inputs, joined, preferred_element_type=jnp.float32)
    return jnp.where(select, coords, 0.0).astype(jnp.bfloat16)


def low_rank(inputs, select, first_factor, second_factor):
    coords = low_coords(inputs, select, first_factor)
    adapter_count, rank_size, outer_width = second_factor.shape
    return jnp.dot(
        coords,
        second_factor.reshape(adapter_count * rank_size, outer_width),
        preferred_element_type=jnp.float32,
    )


def online_step(softmax_state, queries, key_piece, positions, segments, key_pos, lengths):
    running_max, running_sum, weighted = softmax_state
    key_heads = queries.shape[1]
    head_size = queries.shape[3]
    key_part = key_piece[:, : key_heads * head_size].reshape(-1, key_heads, head_size)
    value_part = key_piece[:, key_heads * head_size :].reshape(-1, key_heads, head_size)
    scores = jnp.einsum(
        "tkgd,skd->tkgs", queries, key_part, preferred_element_type=jnp.float32
    ) * head_size ** (-0.5)
    key_seg = segment_of(key_pos, lengths)
    allowed = (
        (key_pos[None, :] <= positions[:, None])
        & (positions[:, None] - key_pos[None, :] < WINDOW)
        & (key_pos[None, :] >= 0)
    )
    allowed = allowed & ((key_seg[None, :] == segments[:, None]) | (key_seg[None, :] == 0))
    scores = jnp.where(allowed[:, None, None, :], scores, NEGATIVE)
    new_max = jnp.maximum(running_max, jnp.max(scores, axis=-1))
    factor = jnp.exp(running_max - new_max)
    weights = jnp.exp(scores - new_max[..., None])
    running_sum = running_sum * factor + jnp.sum(weights, axis=-1)
    weighted = weighted * factor[..., None] + jnp.einsum(
        "tkgs,skd->tkgd",
        weights.astype(jnp.bfloat16),
        value_part,
        preferred_element_type=jnp.float32,
    )
    return (new_max, running_sum, weighted)


def body(
    tokens,
    segment_lengths,
    segment_adapters,
    routes,
    gate_weights,
    attention_gain,
    attention_in,
    sink_logits,
    attention_out,
    expert_gain,
    expert_gate_up,
    expert_down,
    adapter_in_down,
    adapter_in_up,
    adapter_out_down,
    adapter_out_up,
    adapter_expert_down,
    adapter_expert_up,
):
    tok_rows = tokens.shape[0]
    lengths = segment_lengths[0]
    segment_total = lengths.shape[0]
    first_pos = lax.axis_index("exp") * tok_rows
    positions = first_pos + jnp.arange(tok_rows, dtype=jnp.int32)
    segments = segment_of(positions, lengths)
    matches = segments[:, None] == jnp.arange(segment_total, dtype=jnp.int32)[None, :]
    token_adapter = jnp.sum(jnp.where(matches, segment_adapters[0][None, :], 0), axis=1)
    held_factors = (
        lax.all_gather(adapter_in_down, "req", axis=0, tiled=True),
        lax.all_gather(adapter_in_up, "req", axis=0, tiled=True),
        lax.all_gather(adapter_out_down, "req", axis=0, tiled=True),
        lax.all_gather(adapter_out_up, "req", axis=0, tiled=True),
        lax.all_gather(adapter_expert_down, "req", axis=0, tiled=True),
        lax.all_gather(adapter_expert_up, "req", axis=0, tiled=True),
    )
    in_low, in_high, out_low, out_high, expert_low, expert_high = held_factors
    select = adapter_select(token_adapter, in_low.shape[0], in_low.shape[2])
    normed = scaled_norm(tokens, attention_gain)
    full_in, full_out = (
        lax.all_gather(attention_in, "req", axis=1, tiled=True),
        lax.all_gather(attention_out, "req", axis=1, tiled=True),
    )
    base_heads = jnp.dot(normed, full_in, preferred_element_type=jnp.float32)
    projected = (base_heads + low_rank(normed, select, in_low, in_high)).astype(jnp.bfloat16)
    group_size = HEADS // KVH
    queries = projected[:, : HEADS * HD].reshape(tok_rows, KVH, group_size, HD)
    key_value = projected[:, HEADS * HD :]
    sink_grid = jnp.broadcast_to(
        sink_logits.reshape(KVH, group_size)[None], (tok_rows, KVH, group_size)
    )
    initial = (
        sink_grid,
        jnp.ones_like(sink_grid),
        jnp.zeros((tok_rows, KVH, group_size, HD), jnp.float32),
    )
    key_piece = lax.all_gather(key_value, "exp", axis=0, tiled=True)
    piece_rows = key_piece.shape[0]
    block_rows = tok_rows
    block_count = piece_rows // block_rows
    block_rows = 2 * block_rows
    block_count = block_count // 2
    stacked = key_piece.reshape(block_count, block_rows, key_piece.shape[1])

    def visit_block(softmax_state, block_input):
        key_block, block_index = block_input
        block_start = block_index * block_rows
        key_pos = block_start + jnp.arange(block_rows, dtype=jnp.int32)

        def update(state_now):
            return online_step(state_now, queries, key_block, positions, segments, key_pos, lengths)

        def unchanged(state_now):
            return state_now

        needed = jnp.logical_and(
            block_start <= positions[-1], block_start + block_rows - 1 > positions[0] - WINDOW
        )
        return (lax.cond(needed, update, unchanged, softmax_state), None)

    softmax_state = lax.scan(
        visit_block, initial, (stacked, jnp.arange(block_count, dtype=jnp.int32))
    )[0]
    running_max, running_sum, weighted = softmax_state
    attended = (
        (weighted / running_sum[..., None]).reshape(tok_rows, HEADS * HD).astype(jnp.bfloat16)
    )
    base_out = jnp.dot(attended, full_out, preferred_element_type=jnp.float32)
    residual = (
        tokens.astype(jnp.float32) + base_out + low_rank(attended, select, out_low, out_high)
    ).astype(jnp.bfloat16)
    normed_two = scaled_norm(residual, expert_gain)
    low_parts = low_coords(normed_two, select, expert_low)
    top_count = routes.shape[1]
    picked = routes.reshape(-1)
    expert_hot = (picked[:, None] == jnp.arange(EXPERTS, dtype=jnp.int32)[None, :]).astype(
        jnp.int32
    )
    arrival = jnp.sum((jnp.cumsum(expert_hot, axis=0) - 1) * expert_hot, axis=1)
    slot_index = picked * CAP + arrival
    pick_ids = jnp.arange(picked.shape[0], dtype=jnp.int32)
    sources = jnp.full((EXPERTS * CAP,), -1, jnp.int32).at[slot_index].set(pick_ids)
    filled = (sources >= 0)[:, None]
    token_rows = jnp.maximum(sources, 0) // top_count
    peer_count = lax.axis_size("exp")
    local_experts = EXPERTS // peer_count
    send_rows = jnp.where(filled, normed_two[token_rows], 0).reshape(
        peer_count, local_experts, CAP, -1
    )
    send_low = jnp.where(filled, low_parts[token_rows], 0).reshape(
        peer_count, local_experts, CAP, -1
    )
    adapter_bank = jnp.transpose(expert_high, (1, 0, 2, 3)).reshape(
        local_experts, -1, expert_high.shape[3]
    )
    arrived_rows = lax.all_to_all(send_rows, "exp", split_axis=0, concat_axis=0, tiled=True)
    arrived_low = lax.all_to_all(send_low, "exp", split_axis=0, concat_axis=0, tiled=True)
    hidden_width = expert_down.shape[1]
    gate_up = jnp.einsum(
        "necd,edf->necf", arrived_rows, expert_gate_up, preferred_element_type=jnp.float32
    )
    up_part = gate_up[..., hidden_width:] + jnp.einsum(
        "necr,erf->necf", arrived_low, adapter_bank, preferred_element_type=jnp.float32
    )
    hidden = (jax.nn.relu(gate_up[..., :hidden_width]) * up_part).astype(jnp.bfloat16)
    outputs = jnp.einsum(
        "necf,efd->necd", hidden, expert_down, preferred_element_type=jnp.float32
    ).astype(jnp.bfloat16)
    returned = lax.all_to_all(outputs, "exp", split_axis=0, concat_axis=0, tiled=True)
    flat_back = returned.reshape(EXPERTS * CAP, -1)
    per_pick = flat_back[slot_index].astype(jnp.float32).reshape(tok_rows, top_count, -1)
    combined = jnp.sum(gate_weights[:, :, None] * per_pick, axis=1)
    return (residual.astype(jnp.float32) + combined).astype(jnp.bfloat16)


def solution(mesh):
    return jax.shard_map(
        body,
        mesh=mesh,
        in_specs=(
            P(("req", "exp"), None),
            P("req", None),
            P("req", None),
            P(("req", "exp"), None),
            P(("req", "exp"), None),
            P(),
            P(None, "req"),
            P(),
            P(None, "req"),
            P(),
            P("exp", None, None),
            P("exp", None, None),
            P("req", None, None),
            P("req", None, None),
            P("req", None, None),
            P("req", None, None),
            P("req", None, None),
            P("req", "exp", None, None),
        ),
        out_specs=P(("req", "exp"), None),
        check_vma=False,
    )
```

profile of v0, /device:TPU:100, one launch (start us, length us, event | category | flops | bytes accessed | tf_op | source)
XLA Modules:
  0.0 715.5 jit_solution(5835617143987328835)
XLA Ops:
  13.3 15.3 %all_gather.28 = bf16[16,1536,16]{1,2,0:T(8,128)(2,1)S(1)} all-gather(bf16[2,1536,16]{1,2,0:T(8,128)(2,1)} %param.34), channel_id=1, replica_groups=mesh['req'=8,'exp'=16] {'req'}, dimensions={0}, use_global_device_ids=true | all-gather | bytes 884736 | tf_op jit(solution)/shard_map/all_gather | solution.py:108
  28.6 27.7 %all-gather.5.cloned.1.call-done = bf16[1536,2048]{1,0:T(8,128)(2,1)} async-done(((bf16[1536,256]{1,0:T(8,128)(2,1)}), bf16[1536,2048]{1,0:T(8,128)(2,1)}) %all-gather.5.cloned.1.call-update) | async-done | bytes 6291472 | tf_op jit(solution)/shard_map/all_gather | solution.py:119
  56.2 7.5 %fusion.43 = f32[384,2048]{1,0:T(8,128)} fusion(bf16[1536,2048]{1,0:T(8,128)(2,1)} %all-gather.5.cloned.1.call-done, bf16[384,1536]{1,0:T(8,128)(2,1)} %param.22, f32[1536]{0:T(1024)} %param.27, f32[384]{0:T(512)S(1)} %add_rsqrt_fusion.1), kind=kOutput, calls=%fused_computation.66 | convolution fusion | flops 2418278400 | bytes 10624512 | tf_op jit(solution)/shard_map/dot_general | solution.py:122
  63.8 18.2 %all-gather.7.cloned.1.call-done = bf16[16,16,2048]{2,1,0:T(8,128)(2,1)} async-done(((bf16[2,16,2048]{2,1,0:T(8,128)(2,1)}), bf16[16,16,2048]{2,1,0:T(8,128)(2,1)}) %all-gather.7.cloned.1.call-update) | async-done | bytes 1048592 | tf_op jit(solution)/shard_map/all_gather | solution.py:109
  82.0 3.8 add_convert_fusion
  89.6 9.1 %reduce-window.27 = s32[32,12,128]{2,1,0:T(8,128)S(1)} reduce-window(s32[32,12,128]{2,1,0:T(8,128)S(1)} %fusion.45, s32[]{:T(128)} %copy.156), window={size=1x1x128 pad=0_0x0_0x127_0}, to_apply=%region_12.13 | reduce-window | flops 6242304 | bytes 393220 | tf_op jit(solution)/shard_map/reduce-window.2
  99.7 6.2 scatter_custom_fusion
  107.9 14.4 %all_gather.32 = bf16[16,1536,16]{1,2,0:T(8,128)(2,1)} all-gather(bf16[2,1536,16]{1,2,0:T(8,128)(2,1)S(1)} %copy-done.7), channel_id=1, replica_groups=mesh['req'=8,'exp'=16] {'req'}, dimensions={0}, use_global_device_ids=true | all-gather | bytes 884736 | tf_op jit(solution)/shard_map/all_gather | solution.py:110
  122.3 14.9 %all_gather.33 = bf16[16,16,1536]{2,1,0:T(8,128)(2,1)} all-gather(bf16[2,16,1536]{2,1,0:T(8,128)(2,1)S(1)} %copy-done.8), channel_id=1, replica_groups=mesh['req'=8,'exp'=16] {'req'}, dimensions={0}, use_global_device_ids=true | all-gather | bytes 884736 | tf_op jit(solution)/shard_map/all_gather | solution.py:111
  138.7 1.7 copy.109
  140.5 6.1 all-gather.9.cloned.1.call-done
  146.5 8.6 %copy.108 = bf16[8,768,512]{1,2,0:T(8,128)(2,1)} copy(bf16[8,768,512]{2,1,0:T(8,128)(2,1)} %bitcast.111) | data formatting | bytes 12582912 | tf_op jit(solution)/shard_map/while | solution.py:159
  157.1 203.7 %while.18 = (s32[]{:T(128)}, f32[384,2,6]{0,2,1:T(8,128)}, f32[384,2,6]{0,2,1:T(8,128)}, f32[384,2,6,128]{3,0,2,1:T(8,128)S(1)}, s32[8]{0:T(128)}, /*index=5*/s3...) while((s32[]{:T(128)}, f32[384,2,6]{0,2,1:T(8,128)}, ...), condition=%wide.region_11.12_spmd, body=%wide.region_4.11_spmd.sunk | while | flops 1854454528 | bytes 54025088 | solution.py:159
  161.1 29.1 %conditional.2 = ((f32[384,2,6]{0,2,1:T(8,128)}, f32[384,2,6]{0,2,1:T(8,128)}, f32[384,2,6,128]{3,0,2,1:T(8,128)S(1)})) conditional(s32[]{:T(128)} %convert_element_type.156, (f32[384,2,6]{0,2,1:T(8,128)}, f32[384,2,6]{0,2,1:T(8,128)}, f32[384,2,6,128]{3,0,2,1:T(8,128)S(1)}) %tuple.62, (s32[]{:T(128)}, s32[768]{0:T(1024)S(1)}, s32[384]{0:T(512)}, ...), branch_computations={%region_5.5_spmd, %region_6.10_spmd} | conditional | flops 1854454528 | bytes 54021700 | solution.py:157
  163.9 1.7 fusion.10
  167.0 6.5 fusion.2
  173.5 8.2 %fusion.1 = f32[384,2,6]{0,2,1:T(8,128)S(1)} fusion(f32[2,768,384,6]{2,1,3,0:T(8,128)} %get-tuple-element.399, f32[384,2,6]{0,2,1:T(8,128)S(1)} %max.11, pred[384,768]{0,1:T(8,128)(4,1)S(1)} %fusion.10), kind=kLoop, calls=%fused_computation.7 | loop fusion | flops 14151168 | bytes 14487552 | tf_op jit(solution)/shard_map/while/body/eval_jaxpr/cond/branch_1_fun/reduce_sum | solution.py:69
  181.7 7.8 %bitcast_add_fusion = f32[384,2,6,128]{3,0,2,1:T(8,128)S(1)} fusion(f32[384,2,6,128]{3,0,2,1:T(8,128)S(1)} %get-tuple-element.284, bf16[768,2,128,1]{0,2,3,1:T(8,128)(2,1)S(1)} %bitcast.110, f32[2,768,384,6]{2,1,3,0:T(8,128)} %get-tuple-element.399, f32[384,2,6]{0,2,1:T(8,128)S(1)} %max.11, pred[384,768]{0,1:T(8,128)(4,1)S(1)} %fusion.10, ...), kind=kOutput, calls=%fused_computation.11 | convolution fusion | flops 921305088 | bytes 19599360 | tf_op jit(solution)/shard_map/while/body/eval_jaxpr/cond/branch_1_fun/tkgs,skd->tkgd/dot_general | solution.py:70
  194.1 28.6 %conditional.2 = ((f32[384,2,6]{0,2,1:T(8,128)}, f32[384,2,6]{0,2,1:T(8,128)}, f32[384,2,6,128]{3,0,2,1:T(8,128)S(1)})) conditional(s32[]{:T(128)} %convert_element_type.156, (f32[384,2,6]{0,2,1:T(8,128)}, f32[384,2,6]{0,2,1:T(8,128)}, f32[384,2,6,128]{3,0,2,1:T(8,128)S(1)}) %tuple.62, (s32[]{:T(128)}, s32[768]{0:T(1024)S(1)}, s32[384]{0:T(512)}, ...), branch_computations={%region_5.5_spmd, %region_6.10_spmd} | conditional | flops 1854454528 | bytes 54021700 | solution.py:157
  197.0 1.7 fusion.10
  200.0 6.3 fusion.2
  206.3 7.9 %fusion.1 = f32[384,2,6]{0,2,1:T(8,128)S(1)} fusion(f32[2,768,384,6]{2,1,3,0:T(8,128)} %get-tuple-element.399, f32[384,2,6]{0,2,1:T(8,128)S(1)} %max.11, pred[384,768]{0,1:T(8,128)(4,1)S(1)} %fusion.10), kind=kLoop, calls=%fused_computation.7 | loop fusion | flops 14151168 | bytes 14487552 | tf_op jit(solution)/shard_map/while/body/eval_jaxpr/cond/branch_1_fun/reduce_sum | solution.py:69
  214.3 7.8 %bitcast_add_fusion = f32[384,2,6,128]{3,0,2,1:T(8,128)S(1)} fusion(f32[384,2,6,128]{3,0,2,1:T(8,128)S(1)} %get-tuple-element.284, bf16[768,2,128,1]{0,2,3,1:T(8,128)(2,1)S(1)} %bitcast.110, f32[2,768,384,6]{2,1,3,0:T(8,128)} %get-tuple-element.399, f32[384,2,6]{0,2,1:T(8,128)S(1)} %max.11, pred[384,768]{0,1:T(8,128)(4,1)S(1)} %fusion.10, ...), kind=kOutput, calls=%fused_computation.11 | convolution fusion | flops 921305088 | bytes 19599360 | tf_op jit(solution)/shard_map/while/body/eval_jaxpr/cond/branch_1_fun/tkgs,skd->tkgd/dot_general | solution.py:70
  226.7 28.6 %conditional.2 = ((f32[384,2,6]{0,2,1:T(8,128)}, f32[384,2,6]{0,2,1:T(8,128)}, f32[384,2,6,128]{3,0,2,1:T(8,128)S(1)})) conditional(s32[]{:T(128)} %convert_element_type.156, (f32[384,2,6]{0,2,1:T(8,128)}, f32[384,2,6]{0,2,1:T(8,128)}, f32[384,2,6,128]{3,0,2,1:T(8,128)S(1)}) %tuple.62, (s32[]{:T(128)}, s32[768]{0:T(1024)S(1)}, s32[384]{0:T(512)}, ...), branch_computations={%region_5.5_spmd, %region_6.10_spmd} | conditional | flops 1854454528 | bytes 54021700 | solution.py:157
  229.5 1.7 fusion.10
  232.5 6.3 fusion.2
  238.9 7.9 %fusion.1 = f32[384,2,6]{0,2,1:T(8,128)S(1)} fusion(f32[2,768,384,6]{2,1,3,0:T(8,128)} %get-tuple-element.399, f32[384,2,6]{0,2,1:T(8,128)S(1)} %max.11, pred[384,768]{0,1:T(8,128)(4,1)S(1)} %fusion.10), kind=kLoop, calls=%fused_computation.7 | loop fusion | flops 14151168 | bytes 14487552 | tf_op jit(solution)/shard_map/while/body/eval_jaxpr/cond/branch_1_fun/reduce_sum | solution.py:69
  246.9 7.8 %bitcast_add_fusion = f32[384,2,6,128]{3,0,2,1:T(8,128)S(1)} fusion(f32[384,2,6,128]{3,0,2,1:T(8,128)S(1)} %get-tuple-element.284, bf16[768,2,128,1]{0,2,3,1:T(8,128)(2,1)S(1)} %bitcast.110, f32[2,768,384,6]{2,1,3,0:T(8,128)} %get-tuple-element.399, f32[384,2,6]{0,2,1:T(8,128)S(1)} %max.11, pred[384,768]{0,1:T(8,128)(4,1)S(1)} %fusion.10, ...), kind=kOutput, calls=%fused_computation.11 | convolution fusion | flops 921305088 | bytes 19599360 | tf_op jit(solution)/shard_map/while/body/eval_jaxpr/cond/branch_1_fun/tkgs,skd->tkgd/dot_general | solution.py:70
  259.2 28.6 %conditional.2 = ((f32[384,2,6]{0,2,1:T(8,128)}, f32[384,2,6]{0,2,1:T(8,128)}, f32[384,2,6,128]{3,0,2,1:T(8,128)S(1)})) conditional(s32[]{:T(128)} %convert_element_type.156, (f32[384,2,6]{0,2,1:T(8,128)}, f32[384,2,6]{0,2,1:T(8,128)}, f32[384,2,6,128]{3,0,2,1:T(8,128)S(1)}) %tuple.62, (s32[]{:T(128)}, s32[768]{0:T(1024)S(1)}, s32[384]{0:T(512)}, ...), branch_computations={%region_5.5_spmd, %region_6.10_spmd} | conditional | flops 1854454528 | bytes 54021700 | solution.py:157
  262.1 1.7 fusion.10
  265.1 6.3 fusion.2
  271.4 7.9 %fusion.1 = f32[384,2,6]{0,2,1:T(8,128)S(1)} fusion(f32[2,768,384,6]{2,1,3,0:T(8,128)} %get-tuple-element.399, f32[384,2,6]{0,2,1:T(8,128)S(1)} %max.11, pred[384,768]{0,1:T(8,128)(4,1)S(1)} %fusion.10), kind=kLoop, calls=%fused_computation.7 | loop fusion | flops 14151168 | bytes 14487552 | tf_op jit(solution)/shard_map/while/body/eval_jaxpr/cond/branch_1_fun/reduce_sum | solution.py:69
  279.4 7.8 %bitcast_add_fusion = f32[384,2,6,128]{3,0,2,1:T(8,128)S(1)} fusion(f32[384,2,6,128]{3,0,2,1:T(8,128)S(1)} %get-tuple-element.284, bf16[768,2,128,1]{0,2,3,1:T(8,128)(2,1)S(1)} %bitcast.110, f32[2,768,384,6]{2,1,3,0:T(8,128)} %get-tuple-element.399, f32[384,2,6]{0,2,1:T(8,128)S(1)} %max.11, pred[384,768]{0,1:T(8,128)(4,1)S(1)} %fusion.10, ...), kind=kOutput, calls=%fused_computation.11 | convolution fusion | flops 921305088 | bytes 19599360 | tf_op jit(solution)/shard_map/while/body/eval_jaxpr/cond/branch_1_fun/tkgs,skd->tkgd/dot_general | solution.py:70
  291.7 28.6 %conditional.2 = ((f32[384,2,6]{0,2,1:T(8,128)}, f32[384,2,6]{0,2,1:T(8,128)}, f32[384,2,6,128]{3,0,2,1:T(8,128)S(1)})) conditional(s32[]{:T(128)} %convert_element_type.156, (f32[384,2,6]{0,2,1:T(8,128)}, f32[384,2,6]{0,2,1:T(8,128)}, f32[384,2,6,128]{3,0,2,1:T(8,128)S(1)}) %tuple.62, (s32[]{:T(128)}, s32[768]{0:T(1024)S(1)}, s32[384]{0:T(512)}, ...), branch_computations={%region_5.5_spmd, %region_6.10_spmd} | conditional | flops 1854454528 | bytes 54021700 | solution.py:157
  294.6 1.7 fusion.10
  297.6 6.3 fusion.2
  304.0 7.9 %fusion.1 = f32[384,2,6]{0,2,1:T(8,128)S(1)} fusion(f32[2,768,384,6]{2,1,3,0:T(8,128)} %get-tuple-element.399, f32[384,2,6]{0,2,1:T(8,128)S(1)} %max.11, pred[384,768]{0,1:T(8,128)(4,1)S(1)} %fusion.10), kind=kLoop, calls=%fused_computation.7 | loop fusion | flops 14151168 | bytes 14487552 | tf_op jit(solution)/shard_map/while/body/eval_jaxpr/cond/branch_1_fun/reduce_sum | solution.py:69
  311.9 7.8 %bitcast_add_fusion = f32[384,2,6,128]{3,0,2,1:T(8,128)S(1)} fusion(f32[384,2,6,128]{3,0,2,1:T(8,128)S(1)} %get-tuple-element.284, bf16[768,2,128,1]{0,2,3,1:T(8,128)(2,1)S(1)} %bitcast.110, f32[2,768,384,6]{2,1,3,0:T(8,128)} %get-tuple-element.399, f32[384,2,6]{0,2,1:T(8,128)S(1)} %max.11, pred[384,768]{0,1:T(8,128)(4,1)S(1)} %fusion.10, ...), kind=kOutput, calls=%fused_computation.11 | convolution fusion | flops 921305088 | bytes 19599360 | tf_op jit(solution)/shard_map/while/body/eval_jaxpr/cond/branch_1_fun/tkgs,skd->tkgd/dot_general | solution.py:70
  324.3 28.6 %conditional.2 = ((f32[384,2,6]{0,2,1:T(8,128)}, f32[384,2,6]{0,2,1:T(8,128)}, f32[384,2,6,128]{3,0,2,1:T(8,128)S(1)})) conditional(s32[]{:T(128)} %convert_element_type.156, (f32[384,2,6]{0,2,1:T(8,128)}, f32[384,2,6]{0,2,1:T(8,128)}, f32[384,2,6,128]{3,0,2,1:T(8,128)S(1)}) %tuple.62, (s32[]{:T(128)}, s32[768]{0:T(1024)S(1)}, s32[384]{0:T(512)}, ...), branch_computations={%region_5.5_spmd, %region_6.10_spmd} | conditional | flops 1854454528 | bytes 54021700 | solution.py:157
  327.1 1.7 fusion.10
  330.2 6.3 fusion.2
  336.5 7.9 %fusion.1 = f32[384,2,6]{0,2,1:T(8,128)S(1)} fusion(f32[2,768,384,6]{2,1,3,0:T(8,128)} %get-tuple-element.399, f32[384,2,6]{0,2,1:T(8,128)S(1)} %max.11, pred[384,768]{0,1:T(8,128)(4,1)S(1)} %fusion.10), kind=kLoop, calls=%fused_computation.7 | loop fusion | flops 14151168 | bytes 14487552 | tf_op jit(solution)/shard_map/while/body/eval_jaxpr/cond/branch_1_fun/reduce_sum | solution.py:69
  344.5 7.8 %bitcast_add_fusion = f32[384,2,6,128]{3,0,2,1:T(8,128)S(1)} fusion(f32[384,2,6,128]{3,0,2,1:T(8,128)S(1)} %get-tuple-element.284, bf16[768,2,128,1]{0,2,3,1:T(8,128)(2,1)S(1)} %bitcast.110, f32[2,768,384,6]{2,1,3,0:T(8,128)} %get-tuple-element.399, f32[384,2,6]{0,2,1:T(8,128)S(1)} %max.11, pred[384,768]{0,1:T(8,128)(4,1)S(1)} %fusion.10, ...), kind=kOutput, calls=%fused_computation.11 | convolution fusion | flops 921305088 | bytes 19599360 | tf_op jit(solution)/shard_map/while/body/eval_jaxpr/cond/branch_1_fun/tkgs,skd->tkgd/dot_general | solution.py:70
  360.8 2.1 copy.110
  363.0 2.0 divide_convert_fusion
  365.0 5.9 convert_add_fusion.1
  370.9 3.4 fusion.30
  374.8 10.1 %gather_fusion = bf16[2048,1536]{1,0:T(8,128)(2,1)} fusion(bf16[384,1536]{1,0:T(8,128)(2,1)S(1)} %fusion.32, s32[2048]{0:T(1024)S(1)} %copy-done.12), kind=kCustom, calls=%fused_computation | custom fusion | bytes 12591104 | tf_op jit(solution)/shard_map/gather | solution.py:185
  384.9 6.0 broadcast_select_fusion
  390.9 35.5 %all-to-all-start = ((bf16[16,2,64,1536]{3,2,1,0:T(8,128)(2,1)}), bf16[16,2,64,1536]{3,2,1,0:T(8,128)(2,1)}, u32[]{:S(2)}, u32[]{:S(2)}) async-start(bf16[16,2,64,1536]{3,2,1,0:T(8,128)(2,1)} %broadcast_select_fusion), calls=%async_computation | async-start | bytes 12582912 | tf_op jit(solution)/shard_map/all_to_all | solution.py:194
  426.4 13.7 %all_gather.34 = bf16[16,1536,16]{1,2,0:T(8,128)(2,1)S(1)} all-gather(bf16[2,1536,16]{1,2,0:T(8,128)(2,1)S(1)} %copy-done.9), channel_id=1, replica_groups=mesh['req'=8,'exp'=16] {'req'}, dimensions={0}, use_global_device_ids=true | all-gather | bytes 884736 | tf_op jit(solution)/shard_map/all_gather | solution.py:112
  440.1 13.4 %all_gather.35 = bf16[16,2,16,768]{3,2,0,1:T(8,128)(2,1)S(1)} all-gather(bf16[2,2,16,768]{3,2,0,1:T(8,128)(2,1)S(1)} %copy.118), channel_id=1, replica_groups=mesh['req'=8,'exp'=16] {'req'}, dimensions={0}, use_global_device_ids=true | all-gather | bytes 884736 | tf_op jit(solution)/shard_map/all_gather | solution.py:113
  453.9 7.5 %gather_fusion.1 = bf16[2048,256]{1,0:T(8,128)(2,1)S(1)} fusion(bf16[384,256]{1,0:T(8,128)(2,1)S(1)} %fusion.36, s32[2048]{0:T(1024)S(1)} %copy-done.12), kind=kCustom, calls=%fused_computation.1 | custom fusion | bytes 2105344 | tf_op jit(solution)/shard_map/gather | solution.py:188
  462.7 68.9 %all-to-all-done = bf16[16,2,64,1536]{3,2,1,0:T(8,128)(2,1)} async-done(((bf16[16,2,64,1536]{3,2,1,0:T(8,128)(2,1)}), bf16[16,2,64,1536]{3,2,1,0:T(8,128)(2,1)}, u32[]{:S(2)}, u32[]{:S(2)}) %all-to-all-start) | async-done | bytes 6291488 | tf_op jit(solution)/shard_map/all_to_all | solution.py:194
  531.6 6.9 all-to-all-start.1
  538.6 17.0 %fusion.15 = f32[16,2,64,1536]{3,2,0,1:T(8,128)} fusion(bf16[2,1536,1536]{2,1,0:T(8,128)(2,1)} %param.32, bf16[16,2,64,1536]{3,2,1,0:T(8,128)(2,1)} %all-to-all-done), kind=kOutput, calls=%fused_computation.28 | convolution fusion | flops 9663676416 | bytes 28311552 | tf_op jit(solution)/shard_map/necd,edf->necf/dot_general | solution.py:197
  555.6 11.3 %convert_bitcast_fusion = bf16[16,2,64,1536]{3,2,0,1:T(8,128)(2,1)} fusion(bf16[2,768,1536]{2,1,0:T(8,128)(2,1)} %param.33, f32[16,2,64,1536]{3,2,0,1:T(8,128)} %fusion.15, bf16[2,256,768,1]{2,1,3,0:T(8,128)(2,1)S(1)} %bitcast.121, bf16[16,2,64,256]{3,2,1,0:T(8,128)(2,1)S(1)} %all-to-all-done.1), kind=kOutput, calls=%fused_computation.34 | convolution fusion | flops 5646581760 | bytes 25427968 | tf_op jit(solution)/shard_map/necf,efd->necd/dot_general | solution.py:204
  566.9 6.1 copy.120
  573.0 7.7 %all-to-all-start.2 = ((bf16[16,2,64,1536]{3,2,1,0:T(8,128)(2,1)}), bf16[16,2,64,1536]{3,2,1,0:T(8,128)(2,1)}, u32[]{:S(2)}, u32[]{:S(2)}) async-start(bf16[16,2,64,1536]{3,2,1,0:T(8,128)(2,1)} %copy.120), calls=%async_computation.2 | async-start | bytes 12582912 | tf_op jit(solution)/shard_map/all_to_all | solution.py:207
  580.9 88.9 %all-to-all-done.2 = bf16[16,2,64,1536]{3,2,1,0:T(8,128)(2,1)} async-done(((bf16[16,2,64,1536]{3,2,1,0:T(8,128)(2,1)}), bf16[16,2,64,1536]{3,2,1,0:T(8,128)(2,1)}, u32[]{:S(2)}, u32[]{:S(2)}) %all-to-all-start.2) | async-done | bytes 6291488 | tf_op jit(solution)/shard_map/all_to_all | solution.py:207
  669.8 14.0 %gather_fusion.2 = bf16[1536,1536]{1,0:T(8,128)(2,1)} fusion(bf16[2048,1536]{1,0:T(8,128)(2,1)} %bitcast.40, s32[2048]{0:T(1024)S(1)} %pad_clamp_fusion), kind=kCustom, calls=%fused_computation.2 | custom fusion | bytes 9443328 | tf_op jit(solution)/shard_map/gather | solution.py:209
  683.8 9.7 %reshape.299 = f32[384,4,1536]{2,1,0:T(4,128)} reshape(bf16[1536,1536]{1,0:T(8,128)(2,1)} %gather_fusion.2) | data formatting | bytes 14155776 | tf_op jit(solution)/shard_map/convert_element_type | solution.py:209
  693.5 12.3 %multiply_reduce_fusion = f32[384,1536]{1,0:T(8,128)} fusion(f32[384,4,1536]{2,1,0:T(4,128)} %reshape.299, f32[384,4]{1,0:T(8,128)S(1)} %copy.111), kind=kLoop, calls=%fused_computation.27 | loop fusion | flops 4128768 | bytes 11802624 | tf_op jit(solution)/shard_map/reduce_sum | solution.py:210
  705.8 3.0 fusion.33
  (222 shorter events, 67.6 us)
Async XLA Ops:
  6.5 49.7 %all-gather.5.cloned.1.call-start = ((), (), s32[]{:S(2)}) async-start(), calls=%async_computation.3 | async-start | bytes 7077888 | tf_op jit(solution)/shard_map/all_gather | solution.py:119
  7.3 74.7 %all-gather.7.cloned.1.call-start = ((), (), s32[]{:S(2)}) async-start(), calls=%async_computation.4 | async-start | bytes 1179648 | tf_op jit(solution)/shard_map/all_gather | solution.py:109
  8.0 138.5 %all-gather.9.cloned.1.call-start = ((), (), s32[]{:S(2)}) async-start(), calls=%async_computation.5 | async-start | bytes 6684672 | tf_op jit(solution)/shard_map/all_gather | solution.py:135
  9.0 72.9 %copy-start.18 = (s32[256]{0:T(256)}, s32[256]{0:T(256)S(1)}, u32[]{:S(2)}) copy-start(s32[256]{0:T(256)S(1)} %eq.84) | copy-start | bytes 3076
  10.4 0.6 copy-start.6
  11.7 70.3 %copy-start.16 = (s32[384]{0:T(512)}, s32[384]{0:T(512)S(1)}, u32[]{:S(2)}) copy-start(s32[384]{0:T(512)S(1)} %select_reduce_fusion) | copy-start | bytes 4612
  13.3 50.5 %copy-start.21 = (f32[384]{0:T(512)}, f32[384]{0:T(512)S(1)}, u32[]{:S(2)}) copy-start(f32[384]{0:T(512)S(1)} %add_rsqrt_fusion.1) | copy-start | bytes 4612
  28.6 53.4 %copy-start = (bf16[384,1536]{1,0:T(8,128)(2,1)S(1)}, bf16[384,1536]{1,0:T(8,128)(2,1)}, u32[]{:S(2)}) copy-start(bf16[384,1536]{1,0:T(8,128)(2,1)} %param.22) | copy-start | bytes 3538948
  82.0 6.4 copy-start.15
  85.8 22.0 %copy-start.7 = (bf16[2,1536,16]{1,2,0:T(8,128)(2,1)S(1)}, bf16[2,1536,16]{1,2,0:T(8,128)(2,1)}, u32[]{:S(2)}) copy-start(bf16[2,1536,16]{1,2,0:T(8,128)(2,1)} %param.36) | copy-start | bytes 294916
  85.8 36.5 %copy-start.8 = (bf16[2,16,1536]{2,1,0:T(8,128)(2,1)S(1)}, bf16[2,16,1536]{2,1,0:T(8,128)(2,1)}, u32[]{:S(2)}) copy-start(bf16[2,16,1536]{2,1,0:T(8,128)(2,1)} %param.37) | copy-start | bytes 294916
  86.7 278.4 %all-gather.11.cloned.1.call-start = ((), (), s32[]{:S(2)}) async-start(), calls=%async_computation.6 | async-start | bytes 5308416 | tf_op jit(solution)/shard_map/all_gather | solution.py:120
  99.7 22.6 %copy-start.13 = (s32[1536]{0:T(1024)}, s32[1536]{0:T(1024)S(1)}, u32[]{:S(2)}) copy-start(s32[1536]{0:T(1024)S(1)} %fusion.56) | copy-start | bytes 18436
  167.0 6.5 copy-start.3
  173.5 8.2 %copy-start.4 = (f32[384,2,6]{0,2,1:T(8,128)S(1)}, f32[384,2,6]{0,2,1:T(8,128)}, u32[]{:S(2)}) copy-start(f32[384,2,6]{0,2,1:T(8,128)} %get-tuple-element.283) | copy-start | bytes 55300 | tf_op jit(solution)/shard_map/while/body/eval_jaxpr/cond
  181.7 7.9 %copy-start.5 = (f32[384,2,6]{0,2,1:T(8,128)}, f32[384,2,6]{0,2,1:T(8,128)S(1)}, u32[]{:S(2)}) copy-start(f32[384,2,6]{0,2,1:T(8,128)S(1)} %get-tuple-element.479) | copy-start | bytes 55300 | tf_op jit(solution)/shard_map/while/body/eval_jaxpr/cond
  200.0 6.3 copy-start.3
  206.3 7.9 %copy-start.4 = (f32[384,2,6]{0,2,1:T(8,128)S(1)}, f32[384,2,6]{0,2,1:T(8,128)}, u32[]{:S(2)}) copy-start(f32[384,2,6]{0,2,1:T(8,128)} %get-tuple-element.283) | copy-start | bytes 55300 | tf_op jit(solution)/shard_map/while/body/eval_jaxpr/cond
  214.3 7.8 %copy-start.5 = (f32[384,2,6]{0,2,1:T(8,128)}, f32[384,2,6]{0,2,1:T(8,128)S(1)}, u32[]{:S(2)}) copy-start(f32[384,2,6]{0,2,1:T(8,128)S(1)} %get-tuple-element.479) | copy-start | bytes 55300 | tf_op jit(solution)/shard_map/while/body/eval_jaxpr/cond
  232.5 6.3 copy-start.3
  238.9 7.9 %copy-start.4 = (f32[384,2,6]{0,2,1:T(8,128)S(1)}, f32[384,2,6]{0,2,1:T(8,128)}, u32[]{:S(2)}) copy-start(f32[384,2,6]{0,2,1:T(8,128)} %get-tuple-element.283) | copy-start | bytes 55300 | tf_op jit(solution)/shard_map/while/body/eval_jaxpr/cond
  246.8 7.8 %copy-start.5 = (f32[384,2,6]{0,2,1:T(8,128)}, f32[384,2,6]{0,2,1:T(8,128)S(1)}, u32[]{:S(2)}) copy-start(f32[384,2,6]{0,2,1:T(8,128)S(1)} %get-tuple-element.479) | copy-start | bytes 55300 | tf_op jit(solution)/shard_map/while/body/eval_jaxpr/cond
  265.1 6.3 copy-start.3
  271.4 7.9 %copy-start.4 = (f32[384,2,6]{0,2,1:T(8,128)S(1)}, f32[384,2,6]{0,2,1:T(8,128)}, u32[]{:S(2)}) copy-start(f32[384,2,6]{0,2,1:T(8,128)} %get-tuple-element.283) | copy-start | bytes 55300 | tf_op jit(solution)/shard_map/while/body/eval_jaxpr/cond
  279.4 7.8 %copy-start.5 = (f32[384,2,6]{0,2,1:T(8,128)}, f32[384,2,6]{0,2,1:T(8,128)S(1)}, u32[]{:S(2)}) copy-start(f32[384,2,6]{0,2,1:T(8,128)S(1)} %get-tuple-element.479) | copy-start | bytes 55300 | tf_op jit(solution)/shard_map/while/body/eval_jaxpr/cond
  297.6 6.3 copy-start.3
  304.0 7.9 %copy-start.4 = (f32[384,2,6]{0,2,1:T(8,128)S(1)}, f32[384,2,6]{0,2,1:T(8,128)}, u32[]{:S(2)}) copy-start(f32[384,2,6]{0,2,1:T(8,128)} %get-tuple-element.283) | copy-start | bytes 55300 | tf_op jit(solution)/shard_map/while/body/eval_jaxpr/cond
  311.9 7.8 %copy-start.5 = (f32[384,2,6]{0,2,1:T(8,128)}, f32[384,2,6]{0,2,1:T(8,128)S(1)}, u32[]{:S(2)}) copy-start(f32[384,2,6]{0,2,1:T(8,128)S(1)} %get-tuple-element.479) | copy-start | bytes 55300 | tf_op jit(solution)/shard_map/while/body/eval_jaxpr/cond
  330.2 6.3 copy-start.3
  336.5 7.9 %copy-start.4 = (f32[384,2,6]{0,2,1:T(8,128)S(1)}, f32[384,2,6]{0,2,1:T(8,128)}, u32[]{:S(2)}) copy-start(f32[384,2,6]{0,2,1:T(8,128)} %get-tuple-element.283) | copy-start | bytes 55300 | tf_op jit(solution)/shard_map/while/body/eval_jaxpr/cond
  344.5 7.8 %copy-start.5 = (f32[384,2,6]{0,2,1:T(8,128)}, f32[384,2,6]{0,2,1:T(8,128)S(1)}, u32[]{:S(2)}) copy-start(f32[384,2,6]{0,2,1:T(8,128)S(1)} %get-tuple-element.479) | copy-start | bytes 55300 | tf_op jit(solution)/shard_map/while/body/eval_jaxpr/cond
  363.0 2.0 copy-start.1
  365.0 5.9 copy-start.2
  365.0 5.9 copy-start.17
  365.0 5.9 copy-start.19
  370.9 3.5 copy-start.20
  370.9 3.8 copy-start.12
  374.7 10.2 %copy-start.11 = (pred[16,2,64]{2,1,0:T(4,128)(4,1)S(1)}, pred[16,2,64]{2,1,0:T(4,128)(4,1)}, u32[]{:S(2)}) copy-start(pred[16,2,64]{2,1,0:T(4,128)(4,1)} %broadcast_in_dim.122) | copy-start | bytes 6148
  390.9 35.5 %copy-start.10 = (bf16[2,2,16,768]{3,2,1,0:T(8,128)(2,1)S(1)}, bf16[2,2,16,768]{3,2,1,0:T(8,128)(2,1)}, u32[]{:S(2)}) copy-start(bf16[2,2,16,768]{3,2,1,0:T(8,128)(2,1)} %param.39) | copy-start | bytes 294916
  390.9 35.5 %copy-start.9 = (bf16[2,1536,16]{1,2,0:T(8,128)(2,1)S(1)}, bf16[2,1536,16]{1,2,0:T(8,128)(2,1)}, u32[]{:S(2)}) copy-start(bf16[2,1536,16]{1,2,0:T(8,128)(2,1)} %param.38) | copy-start | bytes 294916
  390.9 140.7 %all-to-all-start = ((bf16[16,2,64,1536]{3,2,1,0:T(8,128)(2,1)}), bf16[16,2,64,1536]{3,2,1,0:T(8,128)(2,1)}, u32[]{:S(2)}, u32[]{:S(2)}) async-start(bf16[16,2,64,1536]{3,2,1,0:T(8,128)(2,1)} %broadcast_select_fusion), calls=%async_computation | async-start | bytes 12582912 | tf_op jit(solution)/shard_map/all_to_all | solution.py:194
  531.6 23.9 %all-to-all-start.1 = ((bf16[16,2,64,256]{3,2,1,0:T(8,128)(2,1)}), bf16[16,2,64,256]{3,2,1,0:T(8,128)(2,1)S(1)}, u32[]{:S(2)}, u32[]{:S(2)}) async-start(bf16[16,2,64,256]{3,2,1,0:T(8,128)(2,1)} %broadcast_select_fusion.1), calls=%async_computation.1 | async-start | bytes 2097152 | tf_op jit(solution)/shard_map/all_to_all | solution.py:195
  573.0 7.7 %copy-start.22 = (f32[384,4]{0,1:T(4,128)S(1)}, f32[384,4]{0,1:T(4,128)}, u32[]{:S(2)}) copy-start(f32[384,4]{0,1:T(4,128)} %param.26) | copy-start | bytes 18436
  573.0 7.9 %copy-start.14 = (s32[1536]{0:T(1024)S(1)}, s32[1536]{0:T(1024)}, u32[]{:S(2)}) copy-start(s32[1536]{0:T(1024)} %copy-done.13) | copy-start | bytes 18436
  573.0 96.8 %all-to-all-start.2 = ((bf16[16,2,64,1536]{3,2,1,0:T(8,128)(2,1)}), bf16[16,2,64,1536]{3,2,1,0:T(8,128)(2,1)}, u32[]{:S(2)}, u32[]{:S(2)}) async-start(bf16[16,2,64,1536]{3,2,1,0:T(8,128)(2,1)} %copy.120), calls=%async_computation.2 | async-start | bytes 12582912 | tf_op jit(solution)/shard_map/all_to_all | solution.py:207
Sparse Core Ops, SparseCore 0:
  9.0 47.1 all-gather.4
  58.0 23.9 all-gather.6
  86.8 59.6 all-gather.8
  148.0 35.6 all-gather.10
where the time goes:
time: 724 us; the launch traced here: 716 us
  waiting for transfers between devices  212 us (29%)
  matrix products  134 us (19%)
  local copies, waits for them, and re-layouts  116 us (16%)
  other arithmetic  106 us (15%)
  blocking collectives  71.7 us (10%)
  starting transfers between devices  50.3 us (7%)
  between operations  14.4 us (2%)
  loops' own time  11.5 us (2%)
    all_to_all x1, waiting for transfers between devices, body(): lax.all_to_all(outputs, 'exp', split_axis=0, concat_axis=0, tiled=True)  88.9 us
    all_to_all x1, waiting for transfers between devices, body(): lax.all_to_all(send_rows, 'exp', split_axis=0, concat_axis=0, tiled=True)  68.9 us
    reduce_sum x6, other arithmetic, online_step(): running_sum = running_sum * factor + jnp.sum(weights, axis=-1)  47.7 us
    dot_general x6, matrix products, online_step(): jnp.einsum('tkgs,skd->tkgd', weights.astype(jnp.bfloat16), value_part, pr...  46.8 us
    dot_general x6, matrix products, online_step(): jnp.einsum('tkgd,skd->tkgs', queries, key_part, preferred_element_type=jn...  38.2 us
    all_to_all x1, starting transfers between devices, body(): lax.all_to_all(send_rows, 'exp', split_axis=0, concat_axis=0, tiled=True)  35.5 us
    all_gather x1, waiting for transfers between devices, body(): lax.all_gather(attention_in, 'req', axis=1, tiled=True)  27.7 us
    all_gather x1, waiting for transfers between devices, body(): lax.all_gather(adapter_in_up, 'req', axis=0, tiled=True)  18.2 us
  transfers between devices with their start and end apart: 7, of which 5 were waited for; matrix products, arithmetic and copies ran while one was open for 38% of the time, Pallas kernels for 0%

commit v1 on v0

--- a/solution.py
+++ b/solution.py
@@ -11,6 +11,28 @@
 CAP = 64
 EPSILON = 1e-06
 NEGATIVE = -1e30
+
+
+def joined_along(blocks, dim):
+    lengths = list(blocks.shape[1:])
+    lengths[dim] *= blocks.shape[0]
+    return jnp.moveaxis(blocks, 0, dim).reshape(lengths)
+
+
+def ring_gather(shard, axis, dim):
+    peers = lax.axis_size(axis)
+    pairs = [(i, (i + 1) % peers) for i in range(peers)]
+    back = [(b, a) for a, b in pairs]
+    lower, upper = ([], [])
+    for step in range(peers - 1):
+        if step % 2 == 0:
+            lower.append(lax.ppermute(lower[-1] if lower else shard, axis, pairs))
+        else:
+            upper.append(lax.ppermute(upper[-1] if upper else shard, axis, back))
+    parts = jnp.stack([*lower[::-1], shard, *upper])
+    shift = lax.axis_index(axis) - len(lower)
+    parts = parts[(jnp.arange(peers) - shift) % peers]
+    return joined_along(parts, dim)
 
 
 def scaled_norm(inputs, gain):
@@ -107,7 +129,7 @@
     held_factors = (
         lax.all_gather(adapter_in_down, "req", axis=0, tiled=True),
         lax.all_gather(adapter_in_up, "req", axis=0, tiled=True),
-        lax.all_gather(adapter_out_down, "req", axis=0, tiled=True),
+        ring_gather(adapter_out_down, "req", 0),
         lax.all_gather(adapter_out_up, "req", axis=0, tiled=True),
         lax.all_gather(adapter_expert_down, "req", axis=0, tiled=True),
         lax.all_gather(adapter_expert_up, "req", axis=0, tiled=True),

time: 724 us -> 692 us (0.956)
  local copies, waits for them, and re-layouts: 116 us -> 100 us
  other arithmetic: 106 us -> 91.3 us
  blocking collectives: 71.7 us -> 58.1 us
  starting transfers between devices: 50.3 us -> 57.7 us
    all_gather x1 -> x0, blocking collectives: 14.4 us -> none  [body(): lax.all_gather(adapter_out_down, 'req', axis=0, tiled=True)]
    ppermute x0 -> x7, starting transfers between devices: none -> 9.67 us  [the longest x3 9.06 us: ring_gather(): upper.append(lax.ppermute(upper[-1] if upper else shard, axis, back))]
    ppermute x0 -> x7, waiting for transfers between devices: none -> 7.94 us  [the longest x4 7.69 us: ring_gather(): lower.append(lax.ppermute(lower[-1] if lower else shard, axis, pairs))]
    another operation x8 -> x9, local copies, waits for them, and re-layouts: 8.72 us -> 1.33 us
  transfers between devices with their start and end apart: 7 -> 14, of which waited for: 5 -> 9; matrix products, arithmetic and copies ran while one was open for 38% -> 34% of each run, Pallas kernels for 0% -> 0%
where the time goes in v1:
time: 692 us; the launch traced here: 685 us
  waiting for transfers between devices  217 us (31%)
  matrix products  136 us (20%)
  local copies, waits for them, and re-layouts  100 us (14%)
  other arithmetic  91.3 us (13%)
  blocking collectives  58.1 us (8%)
  starting transfers between devices  57.7 us (8%)
  between operations  14.4 us (2%)
  loops' own time  10.5 us (2%)
    all_to_all x1, waiting for transfers between devices, body(): lax.all_to_all(outputs, 'exp', split_axis=0, concat_axis=0, tiled=True)  88.4 us
    all_to_all x1, waiting for transfers between devices, body(): lax.all_to_all(send_rows, 'exp', split_axis=0, concat_axis=0, tiled=True)  68.3 us
    reduce_sum x6, other arithmetic, online_step(): running_sum = running_sum * factor + jnp.sum(weights, axis=-1)  48.7 us
    dot_general x6, matrix products, online_step(): jnp.einsum('tkgs,skd->tkgd', weights.astype(jnp.bfloat16), value_part, pr...  47.3 us
    dot_general x6, matrix products, online_step(): jnp.einsum('tkgd,skd->tkgs', queries, key_part, preferred_element_type=jn...  38.2 us
    all_to_all x1, starting transfers between devices, body(): lax.all_to_all(send_rows, 'exp', split_axis=0, concat_axis=0, tiled=True)  33.2 us
    all_gather x1, waiting for transfers between devices, body(): lax.all_gather(attention_in, 'req', axis=1, tiled=True)  27.9 us
    all_gather x1, waiting for transfers between devices, body(): lax.all_gather(adapter_in_up, 'req', axis=0, tiled=True)  18.4 us
  transfers between devices with their start and end apart: 14, of which 9 were waited for; matrix products, arithmetic and copies ran while one was open for 34% of the time, Pallas kernels for 0%

profile of v1, /device:TPU:100, one launch (start us, length us, event | category | flops | bytes accessed | tf_op | source)
XLA Modules:
  0.0 685.4 jit_solution(15473120292377303434)
XLA Ops:
  9.9 1.6 fusion.27
  11.5 16.0 %all_gather.25 = bf16[16,1536,16]{1,2,0:T(8,128)(2,1)} all-gather(bf16[2,1536,16]{1,2,0:T(8,128)(2,1)} %param.34), channel_id=1, replica_groups=mesh['req'=8,'exp'=16] {'req'}, dimensions={0}, use_global_device_ids=true | all-gather | bytes 884736 | tf_op jit(solution)/shard_map/all_gather | solution.py:130
  27.5 27.9 %all-gather.5.cloned.1.call-done = bf16[1536,2048]{1,0:T(8,128)(2,1)} async-done(((bf16[1536,256]{1,0:T(8,128)(2,1)}), bf16[1536,2048]{1,0:T(8,128)(2,1)}) %all-gather.5.cloned.1.call-update) | async-done | bytes 6291472 | tf_op jit(solution)/shard_map/all_gather | solution.py:141
  55.4 7.5 %fusion.43 = f32[384,2048]{1,0:T(8,128)} fusion(bf16[1536,2048]{1,0:T(8,128)(2,1)} %all-gather.5.cloned.1.call-done, bf16[384,1536]{1,0:T(8,128)(2,1)} %param.22, f32[1536]{0:T(1024)} %param.27, f32[384]{0:T(512)S(1)} %add_rsqrt_fusion.1), kind=kOutput, calls=%fused_computation.67 | convolution fusion | flops 2418278400 | bytes 10624512 | tf_op jit(solution)/shard_map/dot_general | solution.py:144
  62.9 18.4 %all-gather.7.cloned.1.call-done = bf16[16,16,2048]{2,1,0:T(8,128)(2,1)} async-done(((bf16[2,16,2048]{2,1,0:T(8,128)(2,1)}), bf16[16,16,2048]{2,1,0:T(8,128)(2,1)}) %all-gather.7.cloned.1.call-update) | async-done | bytes 1048592 | tf_op jit(solution)/shard_map/all_gather | solution.py:131
  81.4 4.1 add_convert_fusion
  87.2 2.7 collective-permute-start.4
  90.3 9.1 %reduce-window.27 = s32[32,12,128]{2,1,0:T(8,128)S(1)} reduce-window(s32[32,12,128]{2,1,0:T(8,128)S(1)} %fusion.45, s32[]{:T(128)} %copy.163), window={size=1x1x128 pad=0_0x0_0x127_0}, to_apply=%region_12.13 | reduce-window | flops 6242304 | bytes 393220 | tf_op jit(solution)/shard_map/reduce-window.2
  100.5 6.2 scatter_custom_fusion
  106.7 14.9 %all_gather.29 = bf16[16,16,1536]{2,1,0:T(8,128)(2,1)} all-gather(bf16[2,16,1536]{2,1,0:T(8,128)(2,1)S(1)} %copy-done.4), channel_id=1, replica_groups=mesh['req'=8,'exp'=16] {'req'}, dimensions={0}, use_global_device_ids=true | all-gather | bytes 884736 | tf_op jit(solution)/shard_map/all_gather | solution.py:133
  123.3 3.6 collective-permute-done.1
  126.9 3.0 collective-permute-start.5
  129.9 2.3 collective-permute-done.2
  132.2 3.4 collective-permute-start.6
  135.5 1.9 collective-permute-done.3
  139.5 1.7 copy.107
  142.0 4.1 all-gather.9.cloned.1.call-done
  146.1 8.6 %copy.108 = bf16[8,768,512]{1,2,0:T(8,128)(2,1)} copy(bf16[8,768,512]{2,1,0:T(8,128)(2,1)} %bitcast.132) | data formatting | bytes 12582912 | tf_op jit(solution)/shard_map/while | solution.py:181
  154.8 1.7 broadcast_in_dim.116
  156.5 177.3 %while.18 = (s32[]{:T(128)}, f32[384,2,6]{0,2,1:T(8,128)S(1)}, f32[384,2,6]{0,2,1:T(8,128)S(1)}, f32[384,2,6,128]{3,0,2,1:T(8,128)}, s32[8]{0:T(128)S(1)}, /*ind...) while((s32[]{:T(128)}, f32[384,2,6]{0,2,1:T(8,128)S(1)}, ...), condition=%wide.region_11.12_spmd, body=%wide.region_4.11_spmd.sunk | while | flops 1854454528 | bytes 72678240 | solution.py:181
  158.9 26.8 %conditional.2 = ((f32[384,2,6]{0,2,1:T(8,128)S(1)}, f32[384,2,6]{0,2,1:T(8,128)S(1)}, f32[384,2,6,128]{3,0,2,1:T(8,128)})) conditional(s32[]{:T(128)} %convert_element_type.156, (f32[384,2,6]{0,2,1:T(8,128)S(1)}, f32[384,2,6]{0,2,1:T(8,128)S(1)}, f32[384,2,6,128]{3,0,2,1:T(8,128)}) %tuple.62, (s32[]{:T(128)}, s32[768]{0:T(1024)S(1)}, ...), branch_computations={%region_5.5_spmd, %region_6.10_spmd} | conditional | flops 1854454528 | bytes 72674856 | solution.py:179
  161.4 6.5 fusion.2
  167.9 8.4 %fusion.1 = f32[384,2,6]{0,2,1:T(8,128)S(1)} fusion(f32[2,768,384,6]{2,1,3,0:T(8,128)} %get-tuple-element.399, f32[384,2,6]{0,2,1:T(8,128)S(1)} %max.11, pred[384,768]{0,1:T(8,128)(4,1)S(1)} %fusion.10), kind=kLoop, calls=%fused_computation.8 | loop fusion | flops 14151168 | bytes 14487552 | tf_op jit(solution)/shard_map/while/body/eval_jaxpr/cond/branch_1_fun/reduce_sum | solution.py:91
  176.3 8.0 %bitcast_add_fusion = f32[384,2,6,128]{3,0,2,1:T(8,128)S(1)} fusion(f32[384,2,6,128]{3,0,2,1:T(8,128)S(1)} %copy-done, bf16[768,2,128,1]{0,2,3,1:T(8,128)(2,1)S(1)} %bitcast.131, f32[2,768,384,6]{2,1,3,0:T(8,128)} %get-tuple-element.399, f32[384,2,6]{0,2,1:T(8,128)S(1)} %max.11, pred[384,768]{0,1:T(8,128)(4,1)S(1)} %fusion.10, ...), kind=kOutput, calls=%fused_computation.12 | convolution fusion | flops 921305088 | bytes 19599360 | tf_op jit(solution)/shard_map/while/body/eval_jaxpr/cond/branch_1_fun/tkgs,skd->tkgd/dot_general | solution.py:92
  188.1 26.2 %conditional.2 = ((f32[384,2,6]{0,2,1:T(8,128)S(1)}, f32[384,2,6]{0,2,1:T(8,128)S(1)}, f32[384,2,6,128]{3,0,2,1:T(8,128)})) conditional(s32[]{:T(128)} %convert_element_type.156, (f32[384,2,6]{0,2,1:T(8,128)S(1)}, f32[384,2,6]{0,2,1:T(8,128)S(1)}, f32[384,2,6,128]{3,0,2,1:T(8,128)}) %tuple.62, (s32[]{:T(128)}, s32[768]{0:T(1024)S(1)}, ...), branch_computations={%region_5.5_spmd, %region_6.10_spmd} | conditional | flops 1854454528 | bytes 72674856 | solution.py:179
  190.6 6.3 fusion.2
  196.9 8.1 %fusion.1 = f32[384,2,6]{0,2,1:T(8,128)S(1)} fusion(f32[2,768,384,6]{2,1,3,0:T(8,128)} %get-tuple-element.399, f32[384,2,6]{0,2,1:T(8,128)S(1)} %max.11, pred[384,768]{0,1:T(8,128)(4,1)S(1)} %fusion.10), kind=kLoop, calls=%fused_computation.8 | loop fusion | flops 14151168 | bytes 14487552 | tf_op jit(solution)/shard_map/while/body/eval_jaxpr/cond/branch_1_fun/reduce_sum | solution.py:91
  205.0 7.9 %bitcast_add_fusion = f32[384,2,6,128]{3,0,2,1:T(8,128)S(1)} fusion(f32[384,2,6,128]{3,0,2,1:T(8,128)S(1)} %copy-done, bf16[768,2,128,1]{0,2,3,1:T(8,128)(2,1)S(1)} %bitcast.131, f32[2,768,384,6]{2,1,3,0:T(8,128)} %get-tuple-element.399, f32[384,2,6]{0,2,1:T(8,128)S(1)} %max.11, pred[384,768]{0,1:T(8,128)(4,1)S(1)} %fusion.10, ...), kind=kOutput, calls=%fused_computation.12 | convolution fusion | flops 921305088 | bytes 19599360 | tf_op jit(solution)/shard_map/while/body/eval_jaxpr/cond/branch_1_fun/tkgs,skd->tkgd/dot_general | solution.py:92
  216.8 26.2 %conditional.2 = ((f32[384,2,6]{0,2,1:T(8,128)S(1)}, f32[384,2,6]{0,2,1:T(8,128)S(1)}, f32[384,2,6,128]{3,0,2,1:T(8,128)})) conditional(s32[]{:T(128)} %convert_element_type.156, (f32[384,2,6]{0,2,1:T(8,128)S(1)}, f32[384,2,6]{0,2,1:T(8,128)S(1)}, f32[384,2,6,128]{3,0,2,1:T(8,128)}) %tuple.62, (s32[]{:T(128)}, s32[768]{0:T(1024)S(1)}, ...), branch_computations={%region_5.5_spmd, %region_6.10_spmd} | conditional | flops 1854454528 | bytes 72674856 | solution.py:179
  219.2 6.3 fusion.2
  225.6 8.1 %fusion.1 = f32[384,2,6]{0,2,1:T(8,128)S(1)} fusion(f32[2,768,384,6]{2,1,3,0:T(8,128)} %get-tuple-element.399, f32[384,2,6]{0,2,1:T(8,128)S(1)} %max.11, pred[384,768]{0,1:T(8,128)(4,1)S(1)} %fusion.10), kind=kLoop, calls=%fused_computation.8 | loop fusion | flops 14151168 | bytes 14487552 | tf_op jit(solution)/shard_map/while/body/eval_jaxpr/cond/branch_1_fun/reduce_sum | solution.py:91
  233.7 7.9 %bitcast_add_fusion = f32[384,2,6,128]{3,0,2,1:T(8,128)S(1)} fusion(f32[384,2,6,128]{3,0,2,1:T(8,128)S(1)} %copy-done, bf16[768,2,128,1]{0,2,3,1:T(8,128)(2,1)S(1)} %bitcast.131, f32[2,768,384,6]{2,1,3,0:T(8,128)} %get-tuple-element.399, f32[384,2,6]{0,2,1:T(8,128)S(1)} %max.11, pred[384,768]{0,1:T(8,128)(4,1)S(1)} %fusion.10, ...), kind=kOutput, calls=%fused_computation.12 | convolution fusion | flops 921305088 | bytes 19599360 | tf_op jit(solution)/shard_map/while/body/eval_jaxpr/cond/branch_1_fun/tkgs,skd->tkgd/dot_general | solution.py:92
  245.4 26.2 %conditional.2 = ((f32[384,2,6]{0,2,1:T(8,128)S(1)}, f32[384,2,6]{0,2,1:T(8,128)S(1)}, f32[384,2,6,128]{3,0,2,1:T(8,128)})) conditional(s32[]{:T(128)} %convert_element_type.156, (f32[384,2,6]{0,2,1:T(8,128)S(1)}, f32[384,2,6]{0,2,1:T(8,128)S(1)}, f32[384,2,6,128]{3,0,2,1:T(8,128)}) %tuple.62, (s32[]{:T(128)}, s32[768]{0:T(1024)S(1)}, ...), branch_computations={%region_5.5_spmd, %region_6.10_spmd} | conditional | flops 1854454528 | bytes 72674856 | solution.py:179
  247.9 6.3 fusion.2
  254.2 8.1 %fusion.1 = f32[384,2,6]{0,2,1:T(8,128)S(1)} fusion(f32[2,768,384,6]{2,1,3,0:T(8,128)} %get-tuple-element.399, f32[384,2,6]{0,2,1:T(8,128)S(1)} %max.11, pred[384,768]{0,1:T(8,128)(4,1)S(1)} %fusion.10), kind=kLoop, calls=%fused_computation.8 | loop fusion | flops 14151168 | bytes 14487552 | tf_op jit(solution)/shard_map/while/body/eval_jaxpr/cond/branch_1_fun/reduce_sum | solution.py:91
  262.3 7.9 %bitcast_add_fusion = f32[384,2,6,128]{3,0,2,1:T(8,128)S(1)} fusion(f32[384,2,6,128]{3,0,2,1:T(8,128)S(1)} %copy-done, bf16[768,2,128,1]{0,2,3,1:T(8,128)(2,1)S(1)} %bitcast.131, f32[2,768,384,6]{2,1,3,0:T(8,128)} %get-tuple-element.399, f32[384,2,6]{0,2,1:T(8,128)S(1)} %max.11, pred[384,768]{0,1:T(8,128)(4,1)S(1)} %fusion.10, ...), kind=kOutput, calls=%fused_computation.12 | convolution fusion | flops 921305088 | bytes 19599360 | tf_op jit(solution)/shard_map/while/body/eval_jaxpr/cond/branch_1_fun/tkgs,skd->tkgd/dot_general | solution.py:92
  274.1 26.2 %conditional.2 = ((f32[384,2,6]{0,2,1:T(8,128)S(1)}, f32[384,2,6]{0,2,1:T(8,128)S(1)}, f32[384,2,6,128]{3,0,2,1:T(8,128)})) conditional(s32[]{:T(128)} %convert_element_type.156, (f32[384,2,6]{0,2,1:T(8,128)S(1)}, f32[384,2,6]{0,2,1:T(8,128)S(1)}, f32[384,2,6,128]{3,0,2,1:T(8,128)}) %tuple.62, (s32[]{:T(128)}, s32[768]{0:T(1024)S(1)}, ...), branch_computations={%region_5.5_spmd, %region_6.10_spmd} | conditional | flops 1854454528 | bytes 72674856 | solution.py:179
  276.5 6.3 fusion.2
  282.9 8.1 %fusion.1 = f32[384,2,6]{0,2,1:T(8,128)S(1)} fusion(f32[2,768,384,6]{2,1,3,0:T(8,128)} %get-tuple-element.399, f32[384,2,6]{0,2,1:T(8,128)S(1)} %max.11, pred[384,768]{0,1:T(8,128)(4,1)S(1)} %fusion.10), kind=kLoop, calls=%fused_computation.8 | loop fusion | flops 14151168 | bytes 14487552 | tf_op jit(solution)/shard_map/while/body/eval_jaxpr/cond/branch_1_fun/reduce_sum | solution.py:91
  291.0 7.9 %bitcast_add_fusion = f32[384,2,6,128]{3,0,2,1:T(8,128)S(1)} fusion(f32[384,2,6,128]{3,0,2,1:T(8,128)S(1)} %copy-done, bf16[768,2,128,1]{0,2,3,1:T(8,128)(2,1)S(1)} %bitcast.131, f32[2,768,384,6]{2,1,3,0:T(8,128)} %get-tuple-element.399, f32[384,2,6]{0,2,1:T(8,128)S(1)} %max.11, pred[384,768]{0,1:T(8,128)(4,1)S(1)} %fusion.10, ...), kind=kOutput, calls=%fused_computation.12 | convolution fusion | flops 921305088 | bytes 19599360 | tf_op jit(solution)/shard_map/while/body/eval_jaxpr/cond/branch_1_fun/tkgs,skd->tkgd/dot_general | solution.py:92
  302.7 26.2 %conditional.2 = ((f32[384,2,6]{0,2,1:T(8,128)S(1)}, f32[384,2,6]{0,2,1:T(8,128)S(1)}, f32[384,2,6,128]{3,0,2,1:T(8,128)})) conditional(s32[]{:T(128)} %convert_element_type.156, (f32[384,2,6]{0,2,1:T(8,128)S(1)}, f32[384,2,6]{0,2,1:T(8,128)S(1)}, f32[384,2,6,128]{3,0,2,1:T(8,128)}) %tuple.62, (s32[]{:T(128)}, s32[768]{0:T(1024)S(1)}, ...), branch_computations={%region_5.5_spmd, %region_6.10_spmd} | conditional | flops 1854454528 | bytes 72674856 | solution.py:179
  305.2 6.3 fusion.2
  311.5 8.1 %fusion.1 = f32[384,2,6]{0,2,1:T(8,128)S(1)} fusion(f32[2,768,384,6]{2,1,3,0:T(8,128)} %get-tuple-element.399, f32[384,2,6]{0,2,1:T(8,128)S(1)} %max.11, pred[384,768]{0,1:T(8,128)(4,1)S(1)} %fusion.10), kind=kLoop, calls=%fused_computation.8 | loop fusion | flops 14151168 | bytes 14487552 | tf_op jit(solution)/shard_map/while/body/eval_jaxpr/cond/branch_1_fun/reduce_sum | solution.py:91
  319.6 7.9 %bitcast_add_fusion = f32[384,2,6,128]{3,0,2,1:T(8,128)S(1)} fusion(f32[384,2,6,128]{3,0,2,1:T(8,128)S(1)} %copy-done, bf16[768,2,128,1]{0,2,3,1:T(8,128)(2,1)S(1)} %bitcast.131, f32[2,768,384,6]{2,1,3,0:T(8,128)} %get-tuple-element.399, f32[384,2,6]{0,2,1:T(8,128)S(1)} %max.11, pred[384,768]{0,1:T(8,128)(4,1)S(1)} %fusion.10, ...), kind=kOutput, calls=%fused_computation.12 | convolution fusion | flops 921305088 | bytes 19599360 | tf_op jit(solution)/shard_map/while/body/eval_jaxpr/cond/branch_1_fun/tkgs,skd->tkgd/dot_general | solution.py:92
  333.8 2.2 copy.110
  337.3 6.6 convert_add_fusion.1
  343.8 3.5 fusion.30
  347.8 10.3 %gather_fusion.1 = bf16[2048,1536]{1,0:T(8,128)(2,1)} fusion(bf16[384,1536]{1,0:T(8,128)(2,1)S(1)} %fusion.32, s32[2048]{0:T(1024)S(1)} %fusion.54), kind=kCustom, calls=%fused_computation.1 | custom fusion | bytes 12591104 | tf_op jit(solution)/shard_map/gather | solution.py:207
  358.0 6.0 broadcast_select_fusion
  364.0 33.2 %all-to-all-start = ((bf16[16,2,64,1536]{3,2,1,0:T(8,128)(2,1)}), bf16[16,2,64,1536]{3,2,1,0:T(8,128)(2,1)}, u32[]{:S(2)}, u32[]{:S(2)}) async-start(bf16[16,2,64,1536]{3,2,1,0:T(8,128)(2,1)} %broadcast_select_fusion), calls=%async_computation | async-start | bytes 12582912 | tf_op jit(solution)/shard_map/all_to_all | solution.py:216
  397.3 13.8 %all_gather.30 = bf16[16,1536,16]{1,2,0:T(8,128)(2,1)S(1)} all-gather(bf16[2,1536,16]{1,2,0:T(8,128)(2,1)S(1)} %copy-done.5), channel_id=1, replica_groups=mesh['req'=8,'exp'=16] {'req'}, dimensions={0}, use_global_device_ids=true | all-gather | bytes 884736 | tf_op jit(solution)/shard_map/all_gather | solution.py:134
  411.0 13.4 %all_gather.31 = bf16[16,2,16,768]{3,2,0,1:T(8,128)(2,1)S(1)} all-gather(bf16[2,2,16,768]{3,2,0,1:T(8,128)(2,1)S(1)} %copy.118), channel_id=1, replica_groups=mesh['req'=8,'exp'=16] {'req'}, dimensions={0}, use_global_device_ids=true | all-gather | bytes 884736 | tf_op jit(solution)/shard_map/all_gather | solution.py:135
  424.9 7.5 %gather_fusion.2 = bf16[2048,256]{1,0:T(8,128)(2,1)S(1)} fusion(bf16[384,256]{1,0:T(8,128)(2,1)S(1)} %fusion.36, s32[2048]{0:T(1024)S(1)} %fusion.54), kind=kCustom, calls=%fused_computation.2 | custom fusion | bytes 2105344 | tf_op jit(solution)/shard_map/gather | solution.py:210
  433.7 68.3 %all-to-all-done = bf16[16,2,64,1536]{3,2,1,0:T(8,128)(2,1)} async-done(((bf16[16,2,64,1536]{3,2,1,0:T(8,128)(2,1)}), bf16[16,2,64,1536]{3,2,1,0:T(8,128)(2,1)}, u32[]{:S(2)}, u32[]{:S(2)}) %all-to-all-start) | async-done | bytes 6291488 | tf_op jit(solution)/shard_map/all_to_all | solution.py:216
  502.0 6.9 %all-to-all-start.1 = ((bf16[16,2,64,256]{3,2,1,0:T(8,128)(2,1)}), bf16[16,2,64,256]{3,2,1,0:T(8,128)(2,1)S(1)}, u32[]{:S(2)}, u32[]{:S(2)}) async-start(bf16[16,2,64,256]{3,2,1,0:T(8,128)(2,1)} %broadcast_select_fusion.1), calls=%async_computation.1 | async-start | bytes 2097152 | tf_op jit(solution)/shard_map/all_to_all | solution.py:217
  508.9 17.0 %fusion.15 = f32[16,2,64,1536]{3,2,0,1:T(8,128)} fusion(bf16[2,1536,1536]{2,1,0:T(8,128)(2,1)} %param.32, bf16[16,2,64,1536]{3,2,1,0:T(8,128)(2,1)} %all-to-all-done), kind=kOutput, calls=%fused_computation.29 | convolution fusion | flops 9663676416 | bytes 28311552 | tf_op jit(solution)/shard_map/necd,edf->necf/dot_general | solution.py:219
  525.9 11.3 %convert_bitcast_fusion = bf16[16,2,64,1536]{3,2,0,1:T(8,128)(2,1)} fusion(bf16[2,768,1536]{2,1,0:T(8,128)(2,1)} %param.33, f32[16,2,64,1536]{3,2,0,1:T(8,128)} %fusion.15, bf16[2,256,768,1]{2,1,3,0:T(8,128)(2,1)S(1)} %bitcast.141, bf16[16,2,64,256]{3,2,1,0:T(8,128)(2,1)S(1)} %all-to-all-done.1), kind=kOutput, calls=%fused_computation.35 | convolution fusion | flops 5646581760 | bytes 25427968 | tf_op jit(solution)/shard_map/necf,efd->necd/dot_general | solution.py:226
  537.3 6.1 copy.120
  543.4 7.7 %all-to-all-start.2 = ((bf16[16,2,64,1536]{3,2,1,0:T(8,128)(2,1)}), bf16[16,2,64,1536]{3,2,1,0:T(8,128)(2,1)}, u32[]{:S(2)}, u32[]{:S(2)}) async-start(bf16[16,2,64,1536]{3,2,1,0:T(8,128)(2,1)} %copy.120), calls=%async_computation.2 | async-start | bytes 12582912 | tf_op jit(solution)/shard_map/all_to_all | solution.py:229
  551.3 88.4 %all-to-all-done.2 = bf16[16,2,64,1536]{3,2,1,0:T(8,128)(2,1)} async-done(((bf16[16,2,64,1536]{3,2,1,0:T(8,128)(2,1)}), bf16[16,2,64,1536]{3,2,1,0:T(8,128)(2,1)}, u32[]{:S(2)}, u32[]{:S(2)}) %all-to-all-start.2) | async-done | bytes 6291488 | tf_op jit(solution)/shard_map/all_to_all | solution.py:229
  639.7 14.0 %gather_fusion.3 = bf16[1536,1536]{1,0:T(8,128)(2,1)} fusion(bf16[2048,1536]{1,0:T(8,128)(2,1)} %bitcast.50, s32[2048]{0:T(1024)S(1)} %pad_clamp_fusion), kind=kCustom, calls=%fused_computation.3 | custom fusion | bytes 9443328 | tf_op jit(solution)/shard_map/gather | solution.py:231
  653.7 9.7 %reshape.352 = f32[384,4,1536]{2,1,0:T(4,128)} reshape(bf16[1536,1536]{1,0:T(8,128)(2,1)} %gather_fusion.3) | data formatting | bytes 14155776 | tf_op jit(solution)/shard_map/convert_element_type | solution.py:231
  663.4 12.3 %multiply_reduce_fusion = f32[384,1536]{1,0:T(8,128)} fusion(f32[384,4,1536]{2,1,0:T(4,128)} %reshape.352, f32[384,4]{1,0:T(8,128)S(1)} %copy.111), kind=kLoop, calls=%fused_computation.28 | loop fusion | flops 4128768 | bytes 11802624 | tf_op jit(solution)/shard_map/reduce_sum | solution.py:232
  675.7 3.0 fusion.33
  (222 shorter events, 46.5 us)
Async XLA Ops:
  6.5 48.9 %all-gather.5.cloned.1.call-start = ((), (), s32[]{:S(2)}) async-start(), calls=%async_computation.3 | async-start | bytes 7077888 | tf_op jit(solution)/shard_map/all_gather | solution.py:141
  7.3 74.1 %all-gather.7.cloned.1.call-start = ((), (), s32[]{:S(2)}) async-start(), calls=%async_computation.4 | async-start | bytes 1179648 | tf_op jit(solution)/shard_map/all_gather | solution.py:131
  8.0 138.1 %all-gather.9.cloned.1.call-start = ((), (), s32[]{:S(2)}) async-start(), calls=%async_computation.5 | async-start | bytes 6684672 | tf_op jit(solution)/shard_map/all_gather | solution.py:157
  27.5 53.9 %copy-start.2 = (bf16[384,1536]{1,0:T(8,128)(2,1)S(1)}, bf16[384,1536]{1,0:T(8,128)(2,1)}, u32[]{:S(2)}) copy-start(bf16[384,1536]{1,0:T(8,128)(2,1)} %param.22) | copy-start | bytes 3538948
  27.5 53.9 %copy-start.13 = (f32[1536]{0:T(1024)S(1)}, f32[1536]{0:T(1024)}, u32[]{:S(2)}) copy-start(f32[1536]{0:T(1024)} %param.27) | copy-start | bytes 18436
  81.4 5.5 copy-start.6
  81.4 8.5 %copy-start.10 = (s32[384,4]{0,1:T(4,128)S(1)}, s32[384,4]{0,1:T(4,128)}, u32[]{:S(2)}) copy-start(s32[384,4]{0,1:T(4,128)} %param.25) | copy-start | bytes 18436
  85.5 21.2 %copy-start.4 = (bf16[2,16,1536]{2,1,0:T(8,128)(2,1)S(1)}, bf16[2,16,1536]{2,1,0:T(8,128)(2,1)}, u32[]{:S(2)}) copy-start(bf16[2,16,1536]{2,1,0:T(8,128)(2,1)} %param.37) | copy-start | bytes 294916
  85.5 37.0 %copy-start.15 = (f32[12]{0:T(128)S(1)}, f32[12]{0:T(128)}, u32[]{:S(2)}) copy-start(f32[12]{0:T(128)} %param.29) | copy-start | bytes 148
  86.3 251.0 %all-gather.11.cloned.1.call-start = ((), (), s32[]{:S(2)}) async-start(), calls=%async_computation.6 | async-start | bytes 5308416 | tf_op jit(solution)/shard_map/all_gather | solution.py:142
  86.9 34.7 %collective-permute-start = (bf16[2,1536,16]{1,2,0:T(8,128)(2,1)S(1)}, bf16[2,1536,16]{1,2,0:T(8,128)(2,1)S(1)}, u32[]{:S(2)}, u32[]{:S(2)}) collective-permute-start(bf16[2,1536,16]{1,2,0:T(8,128)(2,1)S(1)} %copy-done.6), channel_id=1, source_target_pairs={{0,16},{16,32},{32,48},{48,64},{64,80},{80,96},{96,112},{112,0},{1... | collective-permute-start | bytes 294920 | tf_op jit(solution)/shard_map/ppermute | solution.py:29
  87.2 39.8 %collective-permute-start.4 = (bf16[2,1536,16]{1,2,0:T(8,128)(2,1)S(1)}, bf16[2,1536,16]{1,2,0:T(8,128)(2,1)S(1)}, u32[]{:S(2)}, u32[]{:S(2)}) collective-permute-start(bf16[2,1536,16]{1,2,0:T(8,128)(2,1)S(1)} %copy-done.6), channel_id=1, source_target_pairs={{16,0},{32,16},{48,32},{64,48},{80,64},{96,80},{112,96},{0,112},{1... | collective-permute-start | bytes 294920 | tf_op jit(solution)/shard_map/ppermute | solution.py:31
  100.4 37.9 %copy-start.8 = (s32[1536]{0:T(1024)}, s32[1536]{0:T(1024)S(1)}, u32[]{:S(2)}) copy-start(s32[1536]{0:T(1024)S(1)} %fusion.56) | copy-start | bytes 18436
  121.6 5.3 collective-permute-start.1
  126.9 5.3 collective-permute-start.2
  126.9 5.2 collective-permute-start.5
  132.1 5.3 collective-permute-start.3
  132.2 5.6 collective-permute-start.6
  146.1 10.4 %copy-start.11 = (s32[1,16]{1,0:T(1,128)S(1)}, s32[1,16]{1,0:T(1,128)}, u32[]{:S(2)}) copy-start(s32[1,16]{1,0:T(1,128)} %param.23) | copy-start | bytes 196
  167.9 8.4 %copy-start = (f32[384,2,6,128]{3,0,2,1:T(8,128)S(1)}, f32[384,2,6,128]{3,0,2,1:T(8,128)}, u32[]{:S(2)}) copy-start(f32[384,2,6,128]{3,0,2,1:T(8,128)} %get-tuple-element.284) | copy-start | bytes 7077892 | tf_op jit(solution)/shard_map/while/body/eval_jaxpr/cond
  184.3 1.5 copy-start.1
  196.9 8.1 %copy-start = (f32[384,2,6,128]{3,0,2,1:T(8,128)S(1)}, f32[384,2,6,128]{3,0,2,1:T(8,128)}, u32[]{:S(2)}) copy-start(f32[384,2,6,128]{3,0,2,1:T(8,128)} %get-tuple-element.284) | copy-start | bytes 7077892 | tf_op jit(solution)/shard_map/while/body/eval_jaxpr/cond
  212.9 1.5 copy-start.1
  225.6 8.1 %copy-start = (f32[384,2,6,128]{3,0,2,1:T(8,128)S(1)}, f32[384,2,6,128]{3,0,2,1:T(8,128)}, u32[]{:S(2)}) copy-start(f32[384,2,6,128]{3,0,2,1:T(8,128)} %get-tuple-element.284) | copy-start | bytes 7077892 | tf_op jit(solution)/shard_map/while/body/eval_jaxpr/cond
  241.5 1.5 copy-start.1
  254.2 8.1 %copy-start = (f32[384,2,6,128]{3,0,2,1:T(8,128)S(1)}, f32[384,2,6,128]{3,0,2,1:T(8,128)}, u32[]{:S(2)}) copy-start(f32[384,2,6,128]{3,0,2,1:T(8,128)} %get-tuple-element.284) | copy-start | bytes 7077892 | tf_op jit(solution)/shard_map/while/body/eval_jaxpr/cond
  270.2 1.5 copy-start.1
  282.9 8.1 %copy-start = (f32[384,2,6,128]{3,0,2,1:T(8,128)S(1)}, f32[384,2,6,128]{3,0,2,1:T(8,128)}, u32[]{:S(2)}) copy-start(f32[384,2,6,128]{3,0,2,1:T(8,128)} %get-tuple-element.284) | copy-start | bytes 7077892 | tf_op jit(solution)/shard_map/while/body/eval_jaxpr/cond
  298.8 1.5 copy-start.1
  311.5 8.1 %copy-start = (f32[384,2,6,128]{3,0,2,1:T(8,128)S(1)}, f32[384,2,6,128]{3,0,2,1:T(8,128)}, u32[]{:S(2)}) copy-start(f32[384,2,6,128]{3,0,2,1:T(8,128)} %get-tuple-element.284) | copy-start | bytes 7077892 | tf_op jit(solution)/shard_map/while/body/eval_jaxpr/cond
  327.5 1.5 copy-start.1
  337.3 6.6 copy-start.3
  343.8 3.6 copy-start.12
  364.0 33.3 %copy-start.7 = (bf16[2,2,16,768]{3,2,1,0:T(8,128)(2,1)S(1)}, bf16[2,2,16,768]{3,2,1,0:T(8,128)(2,1)}, u32[]{:S(2)}) copy-start(bf16[2,2,16,768]{3,2,1,0:T(8,128)(2,1)} %param.39) | copy-start | bytes 294916
  364.0 33.3 %copy-start.5 = (bf16[2,1536,16]{1,2,0:T(8,128)(2,1)S(1)}, bf16[2,1536,16]{1,2,0:T(8,128)(2,1)}, u32[]{:S(2)}) copy-start(bf16[2,1536,16]{1,2,0:T(8,128)(2,1)} %param.38) | copy-start | bytes 294916
  364.0 138.0 %all-to-all-start = ((bf16[16,2,64,1536]{3,2,1,0:T(8,128)(2,1)}), bf16[16,2,64,1536]{3,2,1,0:T(8,128)(2,1)}, u32[]{:S(2)}, u32[]{:S(2)}) async-start(bf16[16,2,64,1536]{3,2,1,0:T(8,128)(2,1)} %broadcast_select_fusion), calls=%async_computation | async-start | bytes 12582912 | tf_op jit(solution)/shard_map/all_to_all | solution.py:216
  502.0 23.9 %all-to-all-start.1 = ((bf16[16,2,64,256]{3,2,1,0:T(8,128)(2,1)}), bf16[16,2,64,256]{3,2,1,0:T(8,128)(2,1)S(1)}, u32[]{:S(2)}, u32[]{:S(2)}) async-start(bf16[16,2,64,256]{3,2,1,0:T(8,128)(2,1)} %broadcast_select_fusion.1), calls=%async_computation.1 | async-start | bytes 2097152 | tf_op jit(solution)/shard_map/all_to_all | solution.py:217
  543.4 7.7 %copy-start.14 = (f32[384,4]{0,1:T(4,128)S(1)}, f32[384,4]{0,1:T(4,128)}, u32[]{:S(2)}) copy-start(f32[384,4]{0,1:T(4,128)} %param.26) | copy-start | bytes 18436
  543.4 7.9 %copy-start.9 = (s32[1536]{0:T(1024)S(1)}, s32[1536]{0:T(1024)}, u32[]{:S(2)}) copy-start(s32[1536]{0:T(1024)} %copy-done.8) | copy-start | bytes 18436
  543.4 96.3 %all-to-all-start.2 = ((bf16[16,2,64,1536]{3,2,1,0:T(8,128)(2,1)}), bf16[16,2,64,1536]{3,2,1,0:T(8,128)(2,1)}, u32[]{:S(2)}, u32[]{:S(2)}) async-start(bf16[16,2,64,1536]{3,2,1,0:T(8,128)(2,1)} %copy.120), calls=%async_computation.2 | async-start | bytes 12582912 | tf_op jit(solution)/shard_map/all_to_all | solution.py:229
Sparse Core Ops, SparseCore 0:
  9.0 46.3 all-gather.4
  57.1 24.2 all-gather.6
  86.4 59.5 all-gather.8
  147.6 35.6 all-gather.10
